TPU v7x, 32 devices: a whole 2x2x4 slice. The times are simulated.
32 devices in a mesh: parts: 2 (over x), ctx: 4 (over z), branch: 4 (over y, core).
Axes of the slice: x: 2, y: 2, z: 4, core: 2. Of those that a mesh axis runs over, the one named last changes fastest.
Arguments:
- prefix_kv: bfloat16 [2, 8192, 1024], P(None, ('parts', 'ctx')), parts along dimension 1
- queries: bfloat16 [512, 8192], P(('parts', 'ctx', 'branch')), parts along dimension 0
- new_kv: bfloat16 [2, 512, 1024], P(None, ('parts', 'ctx', 'branch')), parts along dimension 1, may hold values from -6 to 6
- suffix_kv: bfloat16 [2, 512, 64, 1024], P(None, ('parts', 'ctx', 'branch')), parts along dimension 1, may hold values from -6 to 6
- suffix_len: int32 [512], P(('parts', 'ctx', 'branch')), parts along dimension 0, may hold values from 1 to 64, as said below
- node_kv: bfloat16 [2, 8, 128, 1024], P(None, ('parts', 'branch')), parts along dimension 1, may hold values from -6 to 6
- node_len: int32 [8], P('parts'), parts along dimension 0, may hold values from 1 to 128, as said below
- parent: int32 [8], P('parts'), parts along dimension 0, may hold values from -1 to 2, as said below
- leaf: int32 [512], P(('parts', 'ctx', 'branch')), parts along dimension 0, may hold values from 0 to 3
Outputs:
- context: bfloat16 [512, 8192], P(('parts', 'ctx', 'branch')), parts along dimension 0
There are 2 independent parts, one for each index of `parts`. A program takes and returns all parts, laid end to end along the dimension named above; each array names one. Nothing has to cross between parts.
Inputs may be any that keep to these rules, and one draw needn't show every extreme that they name: `suffix_len`: live tokens stand first in a rollout's suffix; some rollout has all 64. `node_len`: live tokens stand first in a node; some node has all 128. parent[n] is -1 or a node below n; parent[0] is -1.
All inputs are finite; a program needn't handle non-finite values.
Results may differ from a plain program's by a relative error of at most 0.0055.
Values may be sent and summed in bfloat16 or wider, within the bound.
A program may use at most 128 MiB of HBM per device.

v0:
```python
import math

import jax
import jax.numpy as jnp
from jax import lax
from jax.sharding import PartitionSpec as P

HEADS = 64
KV_HEADS = 8
HEAD_DIM = 128
NODE_LEN = 128


def attend(query_block, key_rows, value_rows, live_mask):
    scores = jnp.einsum("bhgd,thd->bhgt", query_block, key_rows, preferred_element_type=jnp.float32)
    scores = scores * query_block.shape[-1] ** (-0.5)
    if live_mask is not None:
        scores = jnp.where(live_mask[:, None, None, :], scores, -jnp.inf)
    maxima = jnp.max(scores, axis=-1)
    anchor = jnp.where(jnp.isfinite(maxima), maxima, 0.0)
    weights = jnp.exp(scores - anchor[..., None])
    totals = jnp.sum(weights, axis=-1)
    mixed = jnp.einsum(
        "bhgt,thd->bhgd",
        weights.astype(jnp.bfloat16),
        value_rows,
        preferred_element_type=jnp.float32,
    )
    return (mixed, maxima, totals)


def combine(first, second):
    mixed_a, maxima_a, totals_a = first
    mixed_b, maxima_b, totals_b = second
    maxima = jnp.maximum(maxima_a, maxima_b)
    anchor = jnp.where(jnp.isfinite(maxima), maxima, 0.0)
    scale_a = jnp.exp(maxima_a - anchor)
    scale_b = jnp.exp(maxima_b - anchor)
    mixed = mixed_a * scale_a[..., None] + mixed_b * scale_b[..., None]
    return (mixed, maxima, totals_a * scale_a + totals_b * scale_b)


def merge_parts(back_mixed, back_maxima, back_totals, ctx_size, rollouts, group):
    back_mixed = back_mixed.reshape(ctx_size, rollouts, KV_HEADS, group, HEAD_DIM)
    back_maxima = back_maxima.reshape(ctx_size, rollouts, KV_HEADS, group)
    back_totals = back_totals.reshape(ctx_size, rollouts, KV_HEADS, group)
    peak = jnp.max(back_maxima, axis=0)
    factors = jnp.exp(back_maxima - peak[None])
    return (
        jnp.sum(back_mixed * factors[..., None], axis=0),
        peak,
        jnp.sum(back_totals * factors, axis=0),
    )


def on_device(prefix_kv, queries, new_kv, suffix_kv, suffix_len, node_kv, node_len, parent, leaf):
    rollouts = queries.shape[0]
    group = HEADS // KV_HEADS
    inverse_root = HEAD_DIM ** (-0.5)
    query_heads = queries.reshape(rollouts, KV_HEADS, group, HEAD_DIM)
    prefix_keys = prefix_kv[0].reshape(-1, KV_HEADS, HEAD_DIM)
    prefix_values = prefix_kv[1].reshape(-1, KV_HEADS, HEAD_DIM)
    node_count = node_len.shape[0]
    node_ids = jnp.arange(node_count, dtype=jnp.int32)
    token_ids = jnp.arange(NODE_LEN, dtype=jnp.int32)
    ctx_size = lax.axis_size("ctx")
    query_rows = lax.all_gather(queries, "ctx", axis=0, tiled=True)
    count = query_rows.shape[0]
    width = math.gcd(count, 16)
    blocks = query_rows.reshape(count // width, width, KV_HEADS, group, HEAD_DIM)

    def one_block(block_rows):
        return attend(block_rows, prefix_keys, prefix_values, None)

    mixed, maxima, totals = lax.map(one_block, blocks)
    fresh = (
        mixed.reshape(count, KV_HEADS, group, HEAD_DIM),
        maxima.reshape(count, KV_HEADS, group),
        totals.reshape(count, KV_HEADS, group),
    )
    held_mixed, held_maxima, held_totals = tuple((made for made in fresh))
    back_mixed, back_maxima, back_totals = (
        lax.all_to_all(held_mixed, "ctx", split_axis=0, concat_axis=0, tiled=True),
        lax.all_to_all(held_maxima, "ctx", split_axis=0, concat_axis=0, tiled=True),
        lax.all_to_all(held_totals, "ctx", split_axis=0, concat_axis=0, tiled=True),
    )
    prefix_state = merge_parts(back_mixed, back_maxima, back_totals, ctx_size, rollouts, group)

    def climb(turn_index, carry):
        current, member = carry
        matched = current[:, None] == node_ids[None, :]
        member = member | matched
        lifted = jnp.sum(jnp.where(matched, parent[None, :], 0), axis=1)
        current = jnp.where(current >= 0, lifted, -1)
        return (current, member)

    start_member = jnp.zeros((leaf.shape[0], node_count), dtype=bool)
    ignored, member = lax.fori_loop(0, node_count, climb, (leaf, start_member))
    shard_piece = lax.all_gather(node_kv, "branch", axis=1, tiled=True)
    count = shard_piece.shape[1]
    live_mask = (member[:, :, None] & (token_ids[None, :] < node_len[:, None])[None, :, :]).reshape(
        member.shape[0], count * NODE_LEN
    )
    key_rows = shard_piece[0].reshape(count * NODE_LEN, KV_HEADS, HEAD_DIM)
    value_rows = shard_piece[1].reshape(count * NODE_LEN, KV_HEADS, HEAD_DIM)
    node_state = combine(
        (
            jnp.zeros((rollouts, KV_HEADS, group, HEAD_DIM), jnp.float32),
            jnp.full((rollouts, KV_HEADS, group), -jnp.inf, jnp.float32),
            jnp.zeros((rollouts, KV_HEADS, group), jnp.float32),
        ),
        attend(query_heads, key_rows, value_rows, live_mask),
    )
    front_state = combine(prefix_state, node_state)
    suffix_keys = suffix_kv[0].reshape(rollouts, -1, KV_HEADS, HEAD_DIM)
    suffix_values = suffix_kv[1].reshape(rollouts, -1, KV_HEADS, HEAD_DIM)
    suffix_scores = (
        jnp.einsum("rhgd,rshd->rhgs", query_heads, suffix_keys, preferred_element_type=jnp.float32)
        * inverse_root
    )
    positions = jnp.arange(suffix_keys.shape[1], dtype=jnp.int32)
    suffix_live = positions[None, :] < suffix_len[:, None]
    suffix_scores = jnp.where(suffix_live[:, None, None, :], suffix_scores, -jnp.inf)
    suffix_peak = jnp.max(suffix_scores, axis=-1)
    suffix_weights = jnp.exp(suffix_scores - suffix_peak[..., None])
    suffix_mixed = jnp.einsum(
        "rhgs,rshd->rhgd",
        suffix_weights.astype(jnp.bfloat16),
        suffix_values,
        preferred_element_type=jnp.float32,
    )
    suffix_state = (suffix_mixed, suffix_peak, jnp.sum(suffix_weights, axis=-1))
    fresh_keys = new_kv[0].reshape(rollouts, KV_HEADS, HEAD_DIM)
    fresh_values = new_kv[1].reshape(rollouts, KV_HEADS, HEAD_DIM).astype(jnp.float32)
    fresh_scores = (
        jnp.einsum("rhgd,rhd->rhg", query_heads, fresh_keys, preferred_element_type=jnp.float32)
        * inverse_root
    )
    fresh_mixed = jnp.broadcast_to(
        fresh_values[:, :, None, :], (rollouts, KV_HEADS, group, HEAD_DIM)
    )
    fresh_state = (fresh_mixed, fresh_scores, jnp.ones_like(fresh_scores))
    state = combine(combine(front_state, suffix_state), fresh_state)
    context = state[0] / state[2][..., None]
    return context.astype(jnp.bfloat16).reshape(rollouts, HEADS * HEAD_DIM)


def solution(mesh):
    return jax.shard_map(
        on_device,
        mesh=mesh,
        in_specs=(
            P(None, ("parts", "ctx"), None),
            P(("parts", "ctx", "branch"), None),
            P(None, ("parts", "ctx", "branch"), None),
            P(None, ("parts", "ctx", "branch"), None, None),
            P(("parts", "ctx", "branch")),
            P(None, ("parts", "branch"), None, None),
            P("parts"),
            P("parts"),
            P(("parts", "ctx", "branch")),
        ),
        out_specs=P(("parts", "ctx", "branch"), None),
        check_vma=False,
    )
```

profile of v0, /device:TPU:0, one launch (start us, length us, event | category | flops | bytes accessed | tf_op | source)
XLA Modules:
  0.0 144.7 jit_solution(16751887422370051576)
XLA Ops:
  8.0 4.0 %fusion.64 = (bf16[1,1024,1024]{2,1,0:T(8,128)(2,1)}, bf16[1,1024,1024]{2,1,0:T(8,128)(2,1)S(1)}) fusion(bf16[2,1024,1024]{2,1,0:T(8,128)(2,1)} %param.13), kind=kLoop, calls=%fused_computation.78 | loop fusion | bytes 8388608 | tf_op jit(solution)/shard_map/slice | solution.py:62
  12.0 2.6 %copy.184 = bf16[1,1024,1024]{1,2,0:T(8,128)(2,1)} copy(bf16[1,1024,1024]{2,1,0:T(8,128)(2,1)S(1)} %get-tuple-element.163) | data formatting | bytes 4194304
  14.6 3.0 %copy.125 = bf16[1024,8,128]{2,0,1:T(8,128)(2,1)S(1)} copy(bf16[1024,8,128]{0,2,1:T(8,128)(2,1)} %bitcast.128) | data formatting | bytes 4194304 | tf_op jit(solution)/shard_map/while | solution.py:75
  17.6 4.0 %copy.185 = bf16[1,1024,1024]{1,2,0:T(8,128)(2,1)} copy(bf16[1,1024,1024]{2,1,0:T(8,128)(2,1)} %get-tuple-element.162) | data formatting | bytes 4194304
  21.6 3.9 %copy.126 = bf16[1024,8,128]{2,0,1:T(8,128)(2,1)} copy(bf16[1024,8,128]{0,2,1:T(8,128)(2,1)} %bitcast.129) | data formatting | bytes 4194304 | tf_op jit(solution)/shard_map/while | solution.py:75
  26.0 13.6 %all-gather.3.cloned.1.call-done = bf16[64,8192]{1,0:T(8,128)(2,1)} async-done(((bf16[16,8192]{1,0:T(8,128)(2,1)}), bf16[64,8192]{1,0:T(8,128)(2,1)}) %all-gather.3.cloned.1.call-update) | async-done | bytes 1048592 | tf_op jit(solution)/shard_map/all_gather | solution.py:67
  39.6 1.5 %copy.190 = bf16[8,8,64,128]{3,2,1,0:T(8,128)(2,1)S(1)} copy(bf16[8,8,64,128]{3,1,2,0:T(8,128)(2,1)} %bitcast.141) | data formatting | bytes 2097152
  41.1 17.2 %while.27 = (s32[]{:T(128)}, f32[4,16,8,8,128]{4,3,2,1,0:T(8,128)}, f32[4,16,8,8]{3,2,1,0:T(8,128)S(1)}, f32[4,16,8,8]{3,2,1,0:T(8,128)}, bf16[4,16,8,8,128]{4,3...) while((s32[]{:T(128)}, f32[4,16,8,8,128]{4,3,2,1,0:T(8,128)}, ...), condition=%wide.region_3.4_spmd, body=%wide.region_0.3_spmd.sunk | while | flops 545259520 | bytes 27288692 | solution.py:75
  59.1 3.3 %all-to-all-start.1 = ((f32[4,1,1024]{2,1,0:T(1,128)}), f32[4,1,1024]{2,1,0:T(1,128)S(1)}, u32[]{:S(2)}, u32[]{:S(2)}) async-start(f32[4,1,1024]{2,1,0:T(1,128)} %reshape.165), calls=%async_computation.1 | async-start | bytes 32768 | tf_op jit(solution)/shard_map/all_to_all | solution.py:84
  62.4 5.0 %fusion.63 = (bf16[1,16,64,1024]{3,2,1,0:T(8,128)(2,1)}, bf16[1,16,64,1024]{3,2,1,0:T(8,128)(2,1)}) fusion(bf16[2,16,64,1024]{3,2,1,0:T(8,128)(2,1)} %param.16), kind=kLoop, calls=%fused_computation.77 | loop fusion | bytes 8388608 | tf_op jit(solution)/shard_map/slice | solution.py:116
  68.1 5.0 %all-to-all-start.2 = ((f32[4,1,1024]{2,1,0:T(1,128)}), f32[4,1,1024]{2,1,0:T(1,128)S(1)}, u32[]{:S(2)}, u32[]{:S(2)}) async-start(f32[4,1,1024]{2,1,0:T(1,128)} %reshape.167), calls=%async_computation.2 | async-start | bytes 32768 | tf_op jit(solution)/shard_map/all_to_all | solution.py:85
  73.3 2.2 %copy.195 = bf16[128,8,8,128]{3,2,1,0:T(8,128)(2,1)S(1)} copy(bf16[128,8,8,128]{3,1,2,0:T(8,128)(2,1)} %bitcast.131) | data formatting | bytes 4194304
  75.6 3.5 %copy.196 = bf16[128,8,8,128]{3,2,1,0:T(8,128)(2,1)} copy(bf16[128,8,8,128]{3,1,2,0:T(8,128)(2,1)} %bitcast.130) | data formatting | bytes 4194304
  79.8 5.2 %all-to-all-start = ((f32[64,8,8,128]{3,2,1,0:T(8,128)}), f32[64,8,8,128]{3,2,1,0:T(8,128)}, u32[]{:S(2)}, u32[]{:S(2)}) async-start(f32[64,8,8,128]{3,2,1,0:T(8,128)} %bitcast.12), calls=%async_computation | async-start | bytes 4194304 | tf_op jit(solution)/shard_map/all_to_all | solution.py:83
  87.4 1.6 %fusion.60 = (bf16[16,8,8,64]{3,2,1,0:T(8,128)(2,1)}, f32[16,8,8]{2,1,0:T(8,128)}) fusion(f32[16,8,8,64]{3,2,1,0:T(8,128)S(1)} %get-tuple-element.179, f32[16,8,8]{2,1,0:T(8,128)S(1)} %get-tuple-element.178), kind=kLoop, calls=%fused_computation.54 | loop fusion | flops 195584 | bytes 401408 | tf_op jit(solution)/shard_map/convert_element_type | solution.py:128
  92.0 1.7 %fusion.65 = (bf16[1,4,128,1024]{3,2,1,0:T(8,128)(2,1)S(1)}, bf16[1,4,128,1024]{3,2,1,0:T(8,128)(2,1)S(1)}) fusion(bf16[2,4,128,1024]{3,2,1,0:T(8,128)(2,1)} %all-gather.5.cloned.1.call-done), kind=kLoop, calls=%fused_computation.79 | loop fusion | bytes 4194304 | tf_op jit(solution)/shard_map/slice | solution.py:104
  94.7 1.3 fusion.66
  96.0 1.5 %copy.133 = f32[16,8,8]{2,1,0:T(8,128)} copy(f32[16,8,8]{0,2,1:T(8,128)} %get-tuple-element.176) | data formatting | bytes 8192 | tf_op jit(solution)/shard_map/reduce_max | solution.py:19
  97.5 1.6 %exponential_multiply_fusion = (f32[16,8,8]{2,1,0:T(8,128)}, f32[16,8,8]{2,1,0:T(8,128)}, f32[16,8,8]{2,1,0:T(8,128)}, f32[16,8,8]{2,1,0:T(8,128)}) fusion(f32[16,8,8]{2,1,0:T(8,128)} %copy.133, f32[16,8,8]{2,1,0:T(8,128)S(1)} %reduce_max.36), kind=kLoop, calls=%fused_computation.72 | loop fusion | flops 6144 | bytes 24576 | tf_op jit(solution)/shard_map/mul;broadcast_in_dim | solution.py:39
  99.0 1.5 %copy.139 = f32[16,8,8]{0,2,1:T(8,128)} copy(f32[16,8,8]{2,1,0:T(8,128)} %get-tuple-element.174) | data formatting | bytes 8192 | tf_op jit(solution)/shard_map/jit(_where)/select_n | solution.py:36
  100.6 2.7 %fusion.25 = (f32[16,8,8]{0,2,1:T(8,128)}, bf16[16,8,8,512]{3,0,2,1:T(8,128)(2,1)}) fusion(f32[16,8,8,512]{3,0,2,1:T(8,128)S(1)} %get-tuple-element.177, f32[16,8,8]{0,2,1:T(8,128)} %copy.139), kind=kLoop, calls=%fused_computation.32 | loop fusion | flops 1571840 | bytes 3153920 | tf_op jit(solution)/shard_map/reduce_sum | solution.py:22
  107.4 25.0 %all-to-all-done = f32[64,8,8,128]{3,2,1,0:T(8,128)} async-done(((f32[64,8,8,128]{3,2,1,0:T(8,128)}), f32[64,8,8,128]{3,2,1,0:T(8,128)}, u32[]{:S(2)}, u32[]{:S(2)}) %all-to-all-start) | async-done | bytes 2097184 | tf_op jit(solution)/shard_map/all_to_all | solution.py:83
  132.4 2.0 %multiply_reduce_fusion = f32[16,8,8,128]{3,2,1,0:T(8,128)S(1)} fusion(f32[4,16,8,8,128]{4,3,2,1,0:T(8,128)} %bitcast.13, f32[4,16,8,8]{3,2,1,0:T(8,128)S(1)} %subtract_exponential_fusion.2), kind=kLoop, calls=%fused_computation.31 | loop fusion | flops 917504 | bytes 2637824 | tf_op jit(solution)/shard_map/reduce_sum | solution.py:50
  134.4 1.5 %fusion.52 = f32[16,8,8,128]{3,2,0,1:T(8,128)S(1)} fusion(bf16[512,8,128,1]{2,1,0,3:T(8,128)(2,1)S(1)} %bitcast.142, bf16[16,8,8,512]{3,0,2,1:T(8,128)(2,1)S(1)} %copy-done.2, f32[16,8,8,128]{3,2,1,0:T(8,128)S(1)} %multiply_reduce_fusion, f32[16,8,8]{2,0,1:T(8,128)S(1)} %copy.147, f32[16,8,8]{2,0,1:T(8,128)S(1)} %copy.145, f32[16,8,8]{2,0,1:T(8,128)S(1)} %copy.143, ...), kind=kOutput, calls=%fused_computation.46 | convolution fusion | flops 135004160 | bytes 3166208 | tf_op jit(solution)/shard_map/bhgt,thd->bhgd/dot_general | solution.py:23
  (121 shorter events, 34.1 us)
Async XLA Ops:
  6.5 33.1 %all-gather.3.cloned.1.call-start = ((), (), s32[]{:S(2)}) async-start(), calls=%async_computation.3 | async-start | bytes 1310720 | tf_op jit(solution)/shard_map/all_gather | solution.py:67
  7.3 84.8 %all-gather.5.cloned.1.call-start = ((), (), s32[]{:S(2)}) async-start(), calls=%async_computation.4 | async-start | bytes 2621440 | tf_op jit(solution)/shard_map/all_gather | solution.py:99
  21.6 3.9 %copy-start.10 = (s32[16]{0:T(128)S(1)}, s32[16]{0:T(128)}, u32[]{:S(2)}) copy-start(s32[16]{0:T(128)} %param.21) | copy-start | bytes 196
  21.6 3.9 %copy-start.13 = (s32[4]{0:T(128)S(1)}, s32[4]{0:T(128)}, u32[]{:S(2)}) copy-start(s32[4]{0:T(128)} %param.20) | copy-start | bytes 52
  41.9 1.6 %copy-start = (bf16[1024,8,128]{2,0,1:T(8,128)(2,1)S(1)}, bf16[1024,8,128]{2,0,1:T(8,128)(2,1)}, u32[]{:S(2)}) copy-start(bf16[1024,8,128]{2,0,1:T(8,128)(2,1)} %get-tuple-element.296) | copy-start | bytes 6291460 | tf_op jit(solution)/shard_map/while
  46.2 1.7 %copy-start = (bf16[1024,8,128]{2,0,1:T(8,128)(2,1)S(1)}, bf16[1024,8,128]{2,0,1:T(8,128)(2,1)}, u32[]{:S(2)}) copy-start(bf16[1024,8,128]{2,0,1:T(8,128)(2,1)} %get-tuple-element.296) | copy-start | bytes 6291460 | tf_op jit(solution)/shard_map/while
  50.6 1.6 %copy-start = (bf16[1024,8,128]{2,0,1:T(8,128)(2,1)S(1)}, bf16[1024,8,128]{2,0,1:T(8,128)(2,1)}, u32[]{:S(2)}) copy-start(bf16[1024,8,128]{2,0,1:T(8,128)(2,1)} %get-tuple-element.296) | copy-start | bytes 6291460 | tf_op jit(solution)/shard_map/while
  54.8 1.6 %copy-start = (bf16[1024,8,128]{2,0,1:T(8,128)(2,1)S(1)}, bf16[1024,8,128]{2,0,1:T(8,128)(2,1)}, u32[]{:S(2)}) copy-start(bf16[1024,8,128]{2,0,1:T(8,128)(2,1)} %get-tuple-element.296) | copy-start | bytes 6291460 | tf_op jit(solution)/shard_map/while
  59.1 9.0 %all-to-all-start.1 = ((f32[4,1,1024]{2,1,0:T(1,128)}), f32[4,1,1024]{2,1,0:T(1,128)S(1)}, u32[]{:S(2)}, u32[]{:S(2)}) async-start(f32[4,1,1024]{2,1,0:T(1,128)} %reshape.165), calls=%async_computation.1 | async-start | bytes 32768 | tf_op jit(solution)/shard_map/all_to_all | solution.py:84
  62.3 5.0 %copy-start.7 = (f32[4,16,8,8]{3,2,1,0:T(8,128)S(1)}, f32[4,16,8,8]{3,2,1,0:T(8,128)}, u32[]{:S(2)}) copy-start(f32[4,16,8,8]{3,2,1,0:T(8,128)} %get-tuple-element.74) | copy-start | bytes 49156
  62.3 10.8 %copy-start.8 = (bf16[2,16,1024]{2,1,0:T(8,128)(2,1)S(1)}, bf16[2,16,1024]{2,1,0:T(8,128)(2,1)}, u32[]{:S(2)}) copy-start(bf16[2,16,1024]{2,1,0:T(8,128)(2,1)} %param.15) | copy-start | bytes 196612
  62.4 10.8 %copy-start.5 = (bf16[16,8192]{1,0:T(8,128)(2,1)S(1)}, bf16[16,8192]{1,0:T(8,128)(2,1)}, u32[]{:S(2)}) copy-start(bf16[16,8192]{1,0:T(8,128)(2,1)} %param.14) | copy-start | bytes 786436
  68.1 11.6 %all-to-all-start.2 = ((f32[4,1,1024]{2,1,0:T(1,128)}), f32[4,1,1024]{2,1,0:T(1,128)S(1)}, u32[]{:S(2)}, u32[]{:S(2)}) async-start(f32[4,1,1024]{2,1,0:T(1,128)} %reshape.167), calls=%async_computation.2 | async-start | bytes 32768 | tf_op jit(solution)/shard_map/all_to_all | solution.py:85
  73.2 13.0 %copy-start.3 = (bf16[2,8,64,128]{3,2,1,0:T(8,128)(2,1)}, bf16[2,8,64,128]{3,2,1,0:T(8,128)(2,1)S(1)}, u32[]{:S(2)}) copy-start(bf16[2,8,64,128]{3,2,1,0:T(8,128)(2,1)S(1)} %copy.193) | copy-start | bytes 786436
  79.8 5.2 %copy-start.11 = (s32[4]{0:T(128)S(1)}, s32[4]{0:T(128)}, u32[]{:S(2)}) copy-start(s32[4]{0:T(128)} %param.19) | copy-start | bytes 52
  79.8 5.3 %copy-start.12 = (s32[16]{0:T(128)S(1)}, s32[16]{0:T(128)}, u32[]{:S(2)}) copy-start(s32[16]{0:T(128)} %param.17) | copy-start | bytes 196
  79.8 52.6 %all-to-all-start = ((f32[64,8,8,128]{3,2,1,0:T(8,128)}), f32[64,8,8,128]{3,2,1,0:T(8,128)}, u32[]{:S(2)}, u32[]{:S(2)}) async-start(f32[64,8,8,128]{3,2,1,0:T(8,128)} %bitcast.12), calls=%async_computation | async-start | bytes 4194304 | tf_op jit(solution)/shard_map/all_to_all | solution.py:83
  93.7 1.0 copy-start.4
  107.3 27.1 %copy-start.2 = (bf16[16,8,8,512]{3,0,2,1:T(8,128)(2,1)S(1)}, bf16[16,8,8,512]{3,0,2,1:T(8,128)(2,1)}, u32[]{:S(2)}) copy-start(bf16[16,8,8,512]{3,0,2,1:T(8,128)(2,1)} %get-tuple-element.165) | copy-start | bytes 3145732
  134.4 1.6 %copy-start.1 = (bf16[128,8,8,128]{3,2,1,0:T(8,128)(2,1)S(1)}, bf16[128,8,8,128]{3,2,1,0:T(8,128)(2,1)}, u32[]{:S(2)}) copy-start(bf16[128,8,8,128]{3,2,1,0:T(8,128)(2,1)} %copy.196) | copy-start | bytes 6291460
  134.4 1.6 %copy-start.6 = (bf16[16,8,8,64]{3,2,1,0:T(8,128)(2,1)S(1)}, bf16[16,8,8,64]{3,2,1,0:T(8,128)(2,1)}, u32[]{:S(2)}) copy-start(bf16[16,8,8,64]{3,2,1,0:T(8,128)(2,1)} %get-tuple-element.168) | copy-start | bytes 393220
  134.4 1.6 %copy-start.9 = (f32[16,8,128]{2,0,1:T(8,128)S(1)}, f32[16,8,128]{2,0,1:T(8,128)}, u32[]{:S(2)}) copy-start(f32[16,8,128]{2,0,1:T(8,128)} %copy.152) | copy-start | bytes 196612
Sparse Core Ops, SparseCore 0:
  8.9 30.6 all-gather.2
  41.2 22.0 all-gather.4
where the time goes:
time: 146 us; the launch traced here: 145 us
  local copies, waits for them, and re-layouts  49.2 us (34%)
  waiting for transfers between devices  40 us (27%)
  other arithmetic  15 us (10%)
  between operations  13.8 us (9%)
  starting transfers between devices  13.5 us (9%)
  matrix products  13.1 us (9%)
    all_to_all x1, waiting for transfers between devices, on_device(): lax.all_to_all(held_mixed, 'ctx', split_axis=0, concat_axis=0, tiled=True)  25 us
    unnamed x40, local copies, waits for them, and re-layouts  17.8 us
    all_gather x1, waiting for transfers between devices, on_device(): query_rows = lax.all_gather(queries, 'ctx', axis=0, tiled=True)  13.6 us
    while x2, local copies, waits for them, and re-layouts, on_device(): mixed, maxima, totals = lax.map(one_block, blocks)  6.96 us
    dynamic_update_slice x8, local copies, waits for them, and re-layouts, on_device(): mixed, maxima, totals = lax.map(one_block, blocks)  6.15 us
    reduce_sum x5, other arithmetic, attend(): totals = jnp.sum(weights, axis=-1)  6.14 us
    dot_general x5, matrix products, attend(): jnp.einsum('bhgt,thd->bhgd', weights.astype(jnp.bfloat16), value_rows, pr...  5.48 us
    all_to_all x1, starting transfers between devices, on_device(): lax.all_to_all(held_mixed, 'ctx', split_axis=0, concat_axis=0, tiled=True)  5.22 us
  transfers between devices with their start and end apart: 5, of which 2 were waited for; matrix products, arithmetic and copies ran while one was open for 49% of the time, Pallas kernels for 0%

commit v1 on v0

v1 whole, which is shorter than its diff:
```python
import functools
import math

import jax
import jax.numpy as jnp
from jax import lax
from jax.experimental import pallas as pl
from jax.experimental.pallas import tpu as pltpu
from jax.sharding import PartitionSpec as P

HEADS = 64
KV_HEADS = 8
HEAD_DIM = 128
NODE_LEN = 128
GROUP = HEADS // KV_HEADS
GW = GROUP * HEAD_DIM
MESH = pl.DeviceIdType.MESH
LOG2E = math.log2(math.e)
COEF = HEAD_DIM ** (-0.5) * LOG2E


def dot_t(keys, rows):
    return lax.dot_general(keys, rows, (((1,), (1,)), ((), ())), preferred_element_type=jnp.float32)


def kernel(
    n, nb, suffix_len, node_len, parent, leaf, q_ref, new_ref, prefix_hbm, suffix_hbm, node_hbm, out_ref,
    prefix, suffix, nodes, vt, qg, o_out, l_out, o_in, l_in, o_loc, l_loc,
    load_sem, q_send, q_recv, r_send, r_recv, l_send, l_recv, n_send, n_recv,
):
    c = lax.axis_index("ctx")
    b = lax.axis_index("branch")
    rollouts = q_ref.shape[0]
    rows = rollouts * GROUP
    node_count = node_len.shape[0]
    suf = suffix.shape[2]

    load_k = pltpu.make_async_copy(prefix_hbm, prefix, load_sem.at[0])
    load_s = pltpu.make_async_copy(suffix_hbm, suffix, load_sem.at[1])
    load_n = pltpu.make_async_copy(node_hbm, nodes.at[b], load_sem.at[2])
    load_k.start()
    load_s.start()
    load_n.start()

    barrier = pltpu.get_barrier_semaphore()
    for k in range(1, n):
        pl.semaphore_signal(barrier, inc=1, device_id={"ctx": lax.rem(c + k, n)}, device_id_type=MESH)
    for k in range(1, nb):
        pl.semaphore_signal(barrier, inc=1, device_id={"branch": lax.rem(b + k, nb)}, device_id_type=MESH)
    pl.semaphore_wait(barrier, n - 1 + nb - 1)

    def cols(g):
        return pl.ds(pl.multiple_of(g * GW, GW), GW)

    def head_cols(g):
        return pl.ds(pl.multiple_of(g * HEAD_DIM, HEAD_DIM), HEAD_DIM)

    def own_copy(side, target, g):
        return pltpu.make_async_remote_copy(
            src_ref=q_ref.at[:, cols(g)], dst_ref=qg.at[c, :, cols(g)],
            send_sem=q_send.at[side, c, g], recv_sem=q_recv.at[c, g],
            device_id={"ctx": target}, device_id_type=MESH)

    def pass_copy(side, src, target, g):
        return pltpu.make_async_remote_copy(
            src_ref=qg.at[src, :, cols(g)], dst_ref=qg.at[src, :, cols(g)],
            send_sem=q_send.at[side, src, g], recv_sem=q_recv.at[src, g],
            device_id={"ctx": target}, device_id_type=MESH)

    def result_copy(peer, slot, g):
        return pltpu.make_async_remote_copy(
            src_ref=o_out.at[peer, g], dst_ref=o_in.at[slot, g],
            send_sem=r_send.at[peer, g], recv_sem=r_recv.at[slot, g],
            device_id={"ctx": peer}, device_id_type=MESH)

    def stat_copy(peer, slot):
        return pltpu.make_async_remote_copy(
            src_ref=l_out.at[peer], dst_ref=l_in.at[slot],
            send_sem=l_send.at[peer], recv_sem=l_recv.at[slot],
            device_id={"ctx": peer}, device_id_type=MESH)

    def node_copy(peer, slot, k):
        return pltpu.make_async_remote_copy(
            src_ref=node_hbm, dst_ref=nodes.at[slot],
            send_sem=n_send.at[k], recv_sem=n_recv.at[slot],
            device_id={"branch": peer}, device_id_type=MESH)

    @pl.loop(0, KV_HEADS)
    def _(g):
        @pl.when(c + 1 < n)
        def _():
            own_copy(0, c + 1, g).start()

        @pl.when(c >= 1)
        def _():
            own_copy(1, c - 1, g).start()

    for k in range(1, nb):
        node_copy(lax.rem(b + k, nb), b, k).start()

    lane = lax.rem(lax.broadcasted_iota(jnp.int32, (1, rows), 1), rollouts)
    lengths = jnp.zeros((1, rows), jnp.int32)
    current = jnp.zeros((1, rows), jnp.int32)
    for r in range(rollouts):
        lengths = jnp.where(lane == r, suffix_len[r], lengths)
        current = jnp.where(lane == r, leaf[r], current)
    limits = [jnp.zeros((1, rows), jnp.int32) for _ in range(node_count)]
    for _ in range(node_count):
        lifted = jnp.full((1, rows), -1, jnp.int32)
        for node in range(node_count):
            hit = current == node
            limits[node] = jnp.where(hit, node_len[node], limits[node])
            lifted = jnp.where(hit, parent[node], lifted)
        current = lifted
    first = lane * suf
    last = first + lengths

    def stack(block):
        return jnp.concatenate(
            [block[:, j * HEAD_DIM:(j + 1) * HEAD_DIM] for j in range(GROUP)], axis=0)

    def prefix_item(query, g, values_t):
        keys = prefix[0, :, head_cols(g)]
        scores = dot_t(keys, query)
        peak = jnp.max(scores, axis=0, keepdims=True) * COEF
        weights = jnp.exp2(scores * COEF - peak)
        total = jnp.sum(weights, axis=0, keepdims=True)
        mixed = jnp.dot(values_t, weights.astype(jnp.bfloat16), preferred_element_type=jnp.float32)
        return mixed / total, peak + jnp.log2(total)

    def serve(src, g, onward, ok):
        pass_copy(0, src, src, g).wait_recv()

        @pl.when(ok)
        def _():
            pass_copy(onward[0], src, onward[1], g).start()

        mixed, stat = prefix_item(stack(qg[src, :, cols(g)]), g, vt[g])
        o_out[src, g] = mixed.astype(jnp.bfloat16)
        l_out[src, pl.ds(g, 1), :] = stat
        result_copy(src, c, g).start()

        @pl.when(g == KV_HEADS - 1)
        def _():
            stat_copy(src, c).start()

    def local_item(g):
        query = stack(q_ref[:, cols(g)])
        pieces = []
        keys = suffix[0, :, :, head_cols(g)].reshape(rollouts * suf, HEAD_DIM)
        token = lax.broadcasted_iota(jnp.int32, (rollouts * suf, rows), 0)
        scores = jnp.where((token >= first) & (token < last), dot_t(keys, query), -jnp.inf)
        pieces.append((scores, suffix[1, :, :, head_cols(g)].reshape(rollouts * suf, HEAD_DIM)))
        spot = lax.broadcasted_iota(jnp.int32, (NODE_LEN, rows), 0)
        for node in range(node_count):
            owner, inner = node // nodes.shape[2], node % nodes.shape[2]
            scores = dot_t(nodes[owner, 0, inner, :, head_cols(g)], query)
            scores = jnp.where(spot < limits[node], scores, -jnp.inf)
            pieces.append((scores, nodes[owner, 1, inner, :, head_cols(g)]))
        spot = lax.broadcasted_iota(jnp.int32, (rollouts, rows), 0)
        scores = jnp.where(spot == lane, dot_t(new_ref[0, :, head_cols(g)], query), -jnp.inf)
        pieces.append((scores, new_ref[1, :, head_cols(g)]))
        peak = functools.reduce(jnp.maximum, [jnp.max(s, axis=0, keepdims=True) for s, _ in pieces]) * COEF
        total, mixed = 0.0, 0.0
        for scores, values in pieces:
            weights = jnp.exp2(scores * COEF - peak)
            total = total + jnp.sum(weights, axis=0, keepdims=True)
            mixed = mixed + lax.dot_general(
                values, weights.astype(jnp.bfloat16), (((0,), (0,)), ((), ())),
                preferred_element_type=jnp.float32)
        return mixed / total, peak + jnp.log2(total)

    load_k.wait()

    @pl.loop(0, KV_HEADS * max(n - 1, 2))
    def _(t):
        d = t // KV_HEADS + 1
        g = lax.rem(t, KV_HEADS)

        @pl.when(d == 1)
        def _():
            values_t = prefix[1, :, head_cols(g)].T
            vt[g] = values_t
            mixed, stat = prefix_item(stack(q_ref[:, cols(g)]), g, values_t)
            o_loc[0, g] = mixed
            l_loc[0, pl.ds(g, 1), :] = stat

        @pl.when(c - d >= 0)
        def _():
            serve(c - d, g, (0, c + 1), c + 1 < n)

        @pl.when(c + d < n)
        def _():
            serve(c + d, g, (1, c - 1), c >= 1)

        @pl.when(t == KV_HEADS)
        def _():
            load_s.wait()
            load_n.wait()
            for k in range(1, nb):
                node_copy(b, lax.rem(b + k, nb), k).wait_recv()

        @pl.when(d == 2)
        def _():
            mixed, stat = local_item(g)
            o_loc[1, g] = mixed
            l_loc[1, pl.ds(g, 1), :] = stat

    for k in range(1, n):
        stat_copy(c, lax.rem(c + k, n)).wait_recv()

    @pl.loop(0, KV_HEADS)
    def _(g):
        stats = [l_loc[0, pl.ds(g, 1), :], l_loc[1, pl.ds(g, 1), :]]
        for k in range(1, n):
            stats.append(l_in[lax.rem(c + k, n), pl.ds(g, 1), :])
        peak = functools.reduce(jnp.maximum, stats)
        shares = [jnp.exp2(stat - peak) for stat in stats]
        scale = 1.0 / functools.reduce(jnp.add, shares)
        mixed = o_loc[0, g] * (shares[0] * scale) + o_loc[1, g] * (shares[1] * scale)
        for k in range(1, n):
            slot = lax.rem(c + k, n)
            result_copy(c, slot, g).wait_recv()
            mixed = mixed + o_in[slot, g].astype(jnp.float32) * (shares[k + 1] * scale)
        done = mixed.T.astype(jnp.bfloat16)
        for j in range(GROUP):
            out_ref[:, pl.ds(pl.multiple_of(g * GW + j * HEAD_DIM, HEAD_DIM), HEAD_DIM)] = (
                done[j * rollouts:(j + 1) * rollouts])

    @pl.loop(0, KV_HEADS)
    def _(g):
        @pl.when(c + 1 < n)
        def _():
            own_copy(0, c + 1, g).wait_send()

        @pl.when(c >= 1)
        def _():
            own_copy(1, c - 1, g).wait_send()

        for d in range(1, n):
            @pl.when((c - d >= 0) & (c + 1 < n))
            def _():
                pass_copy(0, c - d, c + 1, g).wait_send()

            @pl.when((c + d < n) & (c >= 1))
            def _():
                pass_copy(1, c + d, c - 1, g).wait_send()

            result_copy(lax.rem(c + d, n), c, g).wait_send()

    for k in range(1, n):
        stat_copy(lax.rem(c + k, n), c).wait_send()
    for k in range(1, nb):
        node_copy(lax.rem(b + k, nb), b, k).wait_send()


def on_device(n, nb, prefix_kv, queries, new_kv, suffix_kv, suffix_len, node_kv, node_len, parent, leaf):
    rows = queries.shape[0] * GROUP
    smem = pl.BlockSpec(memory_space=pltpu.SMEM)
    vmem = pl.BlockSpec(memory_space=pltpu.VMEM)
    hbm = pl.BlockSpec(memory_space=pl.ANY)
    dma = pltpu.SemaphoreType.DMA
    bf16, f32 = jnp.bfloat16, jnp.float32
    return pl.pallas_call(
        functools.partial(kernel, n, nb),
        out_shape=jax.ShapeDtypeStruct(queries.shape, bf16),
        in_specs=[smem] * 4 + [vmem] * 2 + [hbm] * 3,
        out_specs=vmem,
        scratch_shapes=[
            pltpu.VMEM(prefix_kv.shape, bf16),
            pltpu.VMEM(suffix_kv.shape, bf16),
            pltpu.VMEM((nb,) + node_kv.shape, bf16),
            pltpu.VMEM((KV_HEADS, HEAD_DIM, prefix_kv.shape[1]), bf16),
            pltpu.VMEM((n,) + queries.shape, bf16),
            pltpu.VMEM((n, KV_HEADS, HEAD_DIM, rows), bf16),
            pltpu.VMEM((n, KV_HEADS, rows), f32),
            pltpu.VMEM((n, KV_HEADS, HEAD_DIM, rows), bf16),
            pltpu.VMEM((n, KV_HEADS, rows), f32),
            pltpu.VMEM((2, KV_HEADS, HEAD_DIM, rows), f32),
            pltpu.VMEM((2, KV_HEADS, rows), f32),
            dma((3,)),
            dma((2, n, KV_HEADS)),
            dma((n, KV_HEADS)),
            dma((n, KV_HEADS)),
            dma((n, KV_HEADS)),
            dma((n,)),
            dma((n,)),
            dma((nb,)),
            dma((nb,)),
        ],
        compiler_params=pltpu.CompilerParams(
            collective_id=0, has_side_effects=True, vmem_limit_bytes=50 * 1024 * 1024),
    )(suffix_len, node_len, parent, leaf, queries, new_kv, prefix_kv, suffix_kv, node_kv)


def solution(mesh):
    return jax.shard_map(
        functools.partial(on_device, mesh.shape["ctx"], mesh.shape["branch"]),
        mesh=mesh,
        in_specs=(
            P(None, ("parts", "ctx"), None),
            P(("parts", "ctx", "branch"), None),
            P(None, ("parts", "ctx", "branch"), None),
            P(None, ("parts", "ctx", "branch"), None, None),
            P(("parts", "ctx", "branch")),
            P(None, ("parts", "branch"), None, None),
            P("parts"),
            P("parts"),
            P(("parts", "ctx", "branch")),
        ),
        out_specs=P(("parts", "ctx", "branch"), None),
        check_vma=False,
    )
```

time: 146 us -> 57.2 us (0.39)
  the two profiles are of different devices: /device:TPU:0 before, /device:TPU:1 now
where the time goes in v1:
time: 57.2 us; the launch traced here: 56.9 us
  Pallas kernels  50.8 us (89%)
  local copies, waits for them, and re-layouts  6.15 us (11%)
    pallas_call x1, Pallas kernels, on_device(): pl.pallas_call(functools.partial(kernel, n, nb), out_shape=jax.ShapeDtype...  50.8 us
    unnamed x15, local copies, waits for them, and re-layouts  6.15 us

profile of v1, /device:TPU:1, one launch (start us, length us, event | category | flops | bytes accessed | tf_op | source)
XLA Modules:
  0.0 56.9 jit_solution(1627211015841803686)
XLA Ops:
  0.0 0.0 copy-start
  0.0 1.0 %copy-done = bf16[2,1,128,1024]{3,2,1,0:T(8,128)(2,1)S(1)} copy-done((bf16[2,1,128,1024]{3,2,1,0:T(8,128)(2,1)S(1)}, bf16[2,1,128,1024]{3,2,1,0:T(8,128)(2,1)}, u32[]{:S(2)}) %copy-start) | copy-done | bytes 524312
  1.0 0.0 copy-start.1
  1.0 0.9 %copy-done.1 = bf16[16,8192]{1,0:T(8,128)(2,1)S(1)} copy-done((bf16[16,8192]{1,0:T(8,128)(2,1)S(1)}, bf16[16,8192]{1,0:T(8,128)(2,1)}, u32[]{:S(2)}) %copy-start.1) | copy-done | bytes 262168
  2.0 0.0 copy-start.2
  2.0 0.8 %copy-done.2 = bf16[2,16,1024]{2,1,0:T(8,128)(2,1)S(1)} copy-done((bf16[2,16,1024]{2,1,0:T(8,128)(2,1)S(1)}, bf16[2,16,1024]{2,1,0:T(8,128)(2,1)}, u32[]{:S(2)}) %copy-start.2) | copy-done | bytes 65560
  2.8 0.0 copy-start.3
  2.8 0.7 %copy-done.3 = s32[16]{0:T(128)S(1)} copy-done((s32[16]{0:T(128)S(1)}, s32[16]{0:T(128)}, u32[]{:S(2)}) %copy-start.3) | copy-done | bytes 88
  3.5 0.0 copy-start.4
  3.5 0.7 %copy-done.4 = s32[4]{0:T(128)S(1)} copy-done((s32[4]{0:T(128)S(1)}, s32[4]{0:T(128)}, u32[]{:S(2)}) %copy-start.4) | copy-done | bytes 40
  4.1 0.0 copy-start.5
  4.1 0.7 %copy-done.5 = s32[4]{0:T(128)S(1)} copy-done((s32[4]{0:T(128)S(1)}, s32[4]{0:T(128)}, u32[]{:S(2)}) %copy-start.5) | copy-done | bytes 40
  4.8 0.0 copy-start.6
  4.8 0.7 %copy-done.6 = s32[16]{0:T(128)S(1)} copy-done((s32[16]{0:T(128)S(1)}, s32[16]{0:T(128)}, u32[]{:S(2)}) %copy-start.6) | copy-done | bytes 88
  5.5 50.8 %shard_map.91 = bf16[16,8192]{1,0:T(8,128)(2,1)S(1)} custom-call(s32[16]{0:T(128)S(1)} %copy-done.3, s32[4]{0:T(128)S(1)} %copy-done.4, s32[4]{0:T(128)S(1)} %copy-done.5, s32[16]{0:T(128)S(1)} %copy-done.6, bf16[16,8192]{1,0:T(8,128)(2,1)S(1)} %copy-done.1, bf16[2,16,1024]{2,1,0:T(8,128)(2,1)S(1)} %copy-done.2, bf16[2,1024,1024]{2,1,0:T(8,128)(2,1)} %prefix_hbm.1, ...), custom_call_target="tpu_custom_call" | custom-call | tf_op jit(solution)/shard_map/pallas_call | solution.py:264
  56.2 0.7 %copy.11 = bf16[16,8192]{1,0:T(8,128)(2,1)} copy(bf16[16,8192]{1,0:T(8,128)(2,1)S(1)} %shard_map.91) | data formatting | bytes 524288
Async XLA Ops:
  0.0 1.0 %copy-start = (bf16[2,1,128,1024]{3,2,1,0:T(8,128)(2,1)S(1)}, bf16[2,1,128,1024]{3,2,1,0:T(8,128)(2,1)}, u32[]{:S(2)}) copy-start(bf16[2,1,128,1024]{3,2,1,0:T(8,128)(2,1)} %node_hbm.1) | copy-start | bytes 1572868
  1.0 0.9 %copy-start.1 = (bf16[16,8192]{1,0:T(8,128)(2,1)S(1)}, bf16[16,8192]{1,0:T(8,128)(2,1)}, u32[]{:S(2)}) copy-start(bf16[16,8192]{1,0:T(8,128)(2,1)} %q_ref.1) | copy-start | bytes 786436
  2.0 0.8 %copy-start.2 = (bf16[2,16,1024]{2,1,0:T(8,128)(2,1)S(1)}, bf16[2,16,1024]{2,1,0:T(8,128)(2,1)}, u32[]{:S(2)}) copy-start(bf16[2,16,1024]{2,1,0:T(8,128)(2,1)} %new_ref.1) | copy-start | bytes 196612
  2.8 0.7 %copy-start.3 = (s32[16]{0:T(128)S(1)}, s32[16]{0:T(128)}, u32[]{:S(2)}) copy-start(s32[16]{0:T(128)} %suffix_len.1) | copy-start | bytes 196
  3.5 0.7 %copy-start.4 = (s32[4]{0:T(128)S(1)}, s32[4]{0:T(128)}, u32[]{:S(2)}) copy-start(s32[4]{0:T(128)} %node_len.1) | copy-start | bytes 52
  4.1 0.7 %copy-start.5 = (s32[4]{0:T(128)S(1)}, s32[4]{0:T(128)}, u32[]{:S(2)}) copy-start(s32[4]{0:T(128)} %parent.1) | copy-start | bytes 52
  4.8 0.7 %copy-start.6 = (s32[16]{0:T(128)S(1)}, s32[16]{0:T(128)}, u32[]{:S(2)}) copy-start(s32[16]{0:T(128)} %leaf.1) | copy-start | bytes 196

commit v2 on v1

v2 whole, which is shorter than its diff:
```python
import functools
import math

import jax
import jax.numpy as jnp
from jax import lax
from jax.experimental import pallas as pl
from jax.experimental.pallas import tpu as pltpu
from jax.sharding import PartitionSpec as P

HEADS = 64
KV_HEADS = 8
HEAD_DIM = 128
NODE_LEN = 128
GROUP = HEADS // KV_HEADS
GW = GROUP * HEAD_DIM
MESH = pl.DeviceIdType.MESH
LOG2E = math.log2(math.e)
COEF = HEAD_DIM ** (-0.5) * LOG2E


def dot_t(keys, rows):
    return lax.dot_general(keys, rows, (((1,), (1,)), ((), ())), preferred_element_type=jnp.float32)
LAG = 2


def kernel(
    n, nb, suffix_len_hbm, node_len_hbm, parent_hbm, leaf_hbm, q_hbm, new_hbm, prefix_hbm, suffix_hbm, node_hbm,
    out_ref,
    suffix_len, node_len, parent, leaf, new_ref, prefix, suffix, nodes, vt, qg,
    o_part, l_part, o_out, l_out, o_in, l_in, o_loc, l_loc,
    load_sem, q_send, q_recv, r_send, r_recv, l_send, l_recv, n_send, n_pass, n_recv,
):
    c = lax.axis_index("ctx")
    b = lax.axis_index("branch")
    rollouts = qg.shape[1]
    rows = rollouts * GROUP
    node_count = node_len.shape[0]
    suf = suffix.shape[2]
    chips = nb // 2
    core = lax.rem(b, 2)
    twin = b + 1 - 2 * core

    loads = [
        pltpu.make_async_copy(src, dst, load_sem.at[i])
        for i, (src, dst) in enumerate([
            (q_hbm, qg.at[c]), (prefix_hbm, prefix), (suffix_hbm, suffix), (node_hbm, nodes.at[b]),
            (new_hbm, new_ref), (suffix_len_hbm, suffix_len), (node_len_hbm, node_len),
            (parent_hbm, parent), (leaf_hbm, leaf)])
    ]
    for load in loads:
        load.start()

    barrier = pltpu.get_barrier_semaphore()
    for k in range(1, n):
        pl.semaphore_signal(barrier, inc=1, device_id={"ctx": lax.rem(c + k, n)}, device_id_type=MESH)
    for k in range(1, nb):
        pl.semaphore_signal(barrier, inc=1, device_id={"branch": lax.rem(b + k, nb)}, device_id_type=MESH)
    pl.semaphore_wait(barrier, n - 1 + nb - 1)

    def cols(g):
        return pl.ds(pl.multiple_of(g * GW, GW), GW)

    def head_cols(g):
        return pl.ds(pl.multiple_of(g * HEAD_DIM, HEAD_DIM), HEAD_DIM)

    def own_copy(side, target, g):
        return pltpu.make_async_remote_copy(
            src_ref=q_hbm.at[:, cols(g)], dst_ref=qg.at[c, :, cols(g)],
            send_sem=q_send.at[side, c, g], recv_sem=q_recv.at[c, g],
            device_id={"ctx": target}, device_id_type=MESH)

    def pass_copy(side, src, target, g):
        return pltpu.make_async_remote_copy(
            src_ref=qg.at[src, :, cols(g)], dst_ref=qg.at[src, :, cols(g)],
            send_sem=q_send.at[side, src, g], recv_sem=q_recv.at[src, g],
            device_id={"ctx": target}, device_id_type=MESH)

    def result_copies(dest, side, target, g):
        return (
            pltpu.make_async_remote_copy(
                src_ref=o_out.at[dest, g], dst_ref=o_in.at[side, dest, g],
                send_sem=r_send.at[dest, g], recv_sem=r_recv.at[side, dest, g],
                device_id={"ctx": target}, device_id_type=MESH),
            pltpu.make_async_remote_copy(
                src_ref=l_out.at[dest, g], dst_ref=l_in.at[side, dest, g],
                send_sem=l_send.at[dest, g], recv_sem=l_recv.at[side, dest, g],
                device_id={"ctx": target}, device_id_type=MESH))

    def node_copy(peer, slot, sem):
        return pltpu.make_async_remote_copy(
            src_ref=node_hbm, dst_ref=nodes.at[slot], send_sem=sem, recv_sem=n_recv.at[slot],
            device_id={"branch": peer}, device_id_type=MESH)

    def node_pass(slot, sem):
        return pltpu.make_async_remote_copy(
            src_ref=nodes.at[slot], dst_ref=nodes.at[slot], send_sem=sem, recv_sem=n_recv.at[slot],
            device_id={"branch": twin}, device_id_type=MESH)

    @pl.loop(0, KV_HEADS)
    def _(g):
        @pl.when(c + 1 < n)
        def _():
            own_copy(0, c + 1, g).start()

        @pl.when(c >= 1)
        def _():
            own_copy(1, c - 1, g).start()

    for k in range(1, chips):
        node_copy(lax.rem(b + 2 * k, nb), b, n_send.at[k]).start()
    node_copy(twin, b, n_send.at[0]).start()

    for load in loads[5:]:
        load.wait()
    lane = lax.rem(lax.broadcasted_iota(jnp.int32, (1, rows), 1), rollouts)
    lengths = jnp.zeros((1, rows), jnp.int32)
    current = jnp.zeros((1, rows), jnp.int32)
    for r in range(rollouts):
        lengths = jnp.where(lane == r, suffix_len[r], lengths)
        current = jnp.where(lane == r, leaf[r], current)
    limits = [jnp.zeros((1, rows), jnp.int32) for _ in range(node_count)]
    for _ in range(node_count):
        lifted = jnp.full((1, rows), -1, jnp.int32)
        for node in range(node_count):
            hit = current == node
            limits[node] = jnp.where(hit, node_len[node], limits[node])
            lifted = jnp.where(hit, parent[node], lifted)
        current = lifted
    first = lane * suf
    last = first + lengths

    def stack(block):
        return [block[:, j * HEAD_DIM:(j + 1) * HEAD_DIM] for j in range(GROUP)]

    def ranked(k):
        near = jnp.minimum(c, n - 1 - c)
        by_two = c - (k + 1) // 2 if k % 2 else c + (k + 1) // 2
        single = jnp.where(2 * c > n - 1, c - (k - near), c + (k - near))
        return jnp.where(k <= 2 * near, by_two, single)

    def pump(d, g):
        @pl.when(c - d >= 0)
        def _():
            pass_copy(0, c - d, c - d, g).wait_recv()

            @pl.when(c + 1 < n)
            def _():
                pass_copy(0, c - d, c + 1, g).start()

        @pl.when(c + d < n)
        def _():
            pass_copy(1, c + d, c + d, g).wait_recv()

            @pl.when(c >= 1)
            def _():
                pass_copy(1, c + d, c - 1, g).start()

    def send(dest, g, mixed, stat):
        o_out[dest, g] = mixed.astype(jnp.bfloat16)
        l_out[dest, g] = stat

        @pl.when(dest < c)
        def _():
            for copy in result_copies(dest, 0, c - 1, g):
                copy.start()

        @pl.when(dest > c)
        def _():
            for copy in result_copies(dest, 1, c + 1, g):
                copy.start()

    def emit(dest, g, mixed, stat):
        edge = ((dest < c) & (c == n - 1)) | ((dest > c) & (c == 0))

        @pl.when(edge)
        def _():
            send(dest, g, mixed, stat)

        @pl.when(jnp.logical_not(edge))
        def _():
            o_part[dest, g] = mixed
            l_part[dest, g] = stat

    def pair_item(pair, g):
        for d in (2 * pair, 2 * pair + 1):
            if d:
                pump(d, g)
        one, two = (ranked(2 * pair) if pair else c), ranked(2 * pair + 1)
        query = jnp.concatenate(stack(qg[one, :, cols(g)]) + stack(qg[two, :, cols(g)]), axis=0)
        if pair == 0:
            vt[g] = prefix[1, :, head_cols(g)].T
        scores = dot_t(prefix[0, :, head_cols(g)], query)
        peak = jnp.max(scores, axis=0, keepdims=True) * COEF
        weights = jnp.exp2(scores * COEF - peak)
        total = jnp.sum(weights, axis=0, keepdims=True)
        mixed = jnp.dot(vt[g], weights.astype(jnp.bfloat16), preferred_element_type=jnp.float32)
        mixed = mixed * (1.0 / total)
        stat = peak + jnp.log2(total)
        if pair:
            emit(one, g, mixed[:, :rows], stat[:, :rows])
        else:
            o_loc[0, g] = mixed[:, :rows]
            l_loc[0, g] = stat[:, :rows]
        emit(two, g, mixed[:, rows:], stat[:, rows:])

    def merge(dest, side, g):
        for copy in result_copies(dest, side, dest, g):
            copy.wait_recv()
        stat_a, stat_b = l_part[dest, g], l_in[side, dest, g]
        peak = jnp.maximum(stat_a, stat_b)
        share_a, share_b = jnp.exp2(stat_a - peak), jnp.exp2(stat_b - peak)
        total = share_a + share_b
        scale = 1.0 / total
        mixed = o_part[dest, g] * (share_a * scale) + o_in[side, dest, g].astype(jnp.float32) * (share_b * scale)
        send(dest, g, mixed, peak + jnp.log2(total))

    def local_item(g):
        query = jnp.concatenate(stack(qg[c, :, cols(g)]), axis=0)
        pieces = []
        keys = suffix[0, :, :, head_cols(g)].reshape(rollouts * suf, HEAD_DIM)
        token = lax.broadcasted_iota(jnp.int32, (rollouts * suf, rows), 0)
        scores = jnp.where((token >= first) & (token < last), dot_t(keys, query), -jnp.inf)
        pieces.append((scores, suffix[1, :, :, head_cols(g)].reshape(rollouts * suf, HEAD_DIM)))
        spot = lax.broadcasted_iota(jnp.int32, (NODE_LEN, rows), 0)
        for node in range(node_count):
            owner, inner = node // nodes.shape[2], node % nodes.shape[2]
            scores = dot_t(nodes[owner, 0, inner, :, head_cols(g)], query)
            scores = jnp.where(spot < limits[node], scores, -jnp.inf)
            pieces.append((scores, nodes[owner, 1, inner, :, head_cols(g)]))
        spot = lax.broadcasted_iota(jnp.int32, (rollouts, rows), 0)
        scores = jnp.where(spot == lane, dot_t(new_ref[0, :, head_cols(g)], query), -jnp.inf)
        pieces.append((scores, new_ref[1, :, head_cols(g)]))
        peak = functools.reduce(jnp.maximum, [jnp.max(s, axis=0, keepdims=True) for s, _ in pieces]) * COEF
        total, mixed = 0.0, 0.0
        for scores, values in pieces:
            weights = jnp.exp2(scores * COEF - peak)
            total = total + jnp.sum(weights, axis=0, keepdims=True)
            mixed = mixed + lax.dot_general(
                values, weights.astype(jnp.bfloat16), (((0,), (0,)), ((), ())),
                preferred_element_type=jnp.float32)
        return mixed / total, peak + jnp.log2(total)

    loads[0].wait()
    loads[1].wait()
    for pair in range(n // 2 - 1):
        @pl.loop(0, KV_HEADS)
        def _(g):
            pair_item(pair, g)

    @pl.loop(0, max(2 * KV_HEADS, KV_HEADS + LAG * (n - 2)))
    def _(t):
        @pl.when(t < KV_HEADS)
        def _():
            pair_item(n // 2 - 1, t)

        for ring in range(1, n - 1):
            g = t - LAG * ring

            @pl.when((g >= 0) & (g < KV_HEADS))
            def _():
                @pl.when(c == n - 1 - ring)
                def _():
                    for dest in range(n - 1 - ring):
                        merge(dest, 0, g)

                @pl.when(c == ring)
                def _():
                    for dest in range(ring + 1, n):
                        merge(dest, 1, g)

        @pl.when(t == KV_HEADS - 2)
        def _():
            for k in range(1, chips):
                slot = lax.rem(b + 2 * k, nb)
                node_pass(slot, n_pass.at[k]).wait_recv()
                node_pass(slot, n_pass.at[k]).start()

        @pl.when(t == KV_HEADS)
        def _():
            for load in loads[2:5]:
                load.wait()
            for k in range(chips):
                slot = lax.rem(twin + 2 * k, nb)
                node_pass(slot, n_pass.at[k]).wait_recv()

        @pl.when((t >= KV_HEADS) & (t < 2 * KV_HEADS))
        def _():
            g = t - KV_HEADS
            mixed, stat = local_item(g)
            o_loc[1, g] = mixed
            l_loc[1, g] = stat

    @pl.loop(0, KV_HEADS)
    def _(g):
        for side, alone in ((0, c == n - 1), (1, c == 0)):
            @pl.when(alone)
            def _():
                o_in[side, c, g] = jnp.zeros((HEAD_DIM, rows), jnp.bfloat16)
                l_in[side, c, g] = jnp.full((1, rows), -jnp.inf, jnp.float32)

            @pl.when(jnp.logical_not(alone))
            def _():
                for copy in result_copies(c, side, c, g):
                    copy.wait_recv()

        stats = [l_loc[0, g], l_loc[1, g], l_in[0, c, g], l_in[1, c, g]]
        parts = [o_loc[0, g], o_loc[1, g], o_in[0, c, g], o_in[1, c, g]]
        peak = functools.reduce(jnp.maximum, stats)
        shares = [jnp.exp2(stat - peak) for stat in stats]
        scale = 1.0 / functools.reduce(jnp.add, shares)
        mixed = functools.reduce(
            jnp.add, [part.astype(jnp.float32) * (share * scale) for part, share in zip(parts, shares)])
        done = mixed.T.astype(jnp.bfloat16)
        for j in range(GROUP):
            out_ref[:, pl.ds(pl.multiple_of(g * GW + j * HEAD_DIM, HEAD_DIM), HEAD_DIM)] = (
                done[j * rollouts:(j + 1) * rollouts])

    @pl.loop(0, KV_HEADS)
    def _(g):
        @pl.when(c + 1 < n)
        def _():
            own_copy(0, c + 1, g).wait_send()

        @pl.when(c >= 1)
        def _():
            own_copy(1, c - 1, g).wait_send()

        for d in range(1, n):
            @pl.when((c - d >= 0) & (c + 1 < n))
            def _():
                pass_copy(0, c - d, c + 1, g).wait_send()

            @pl.when((c + d < n) & (c >= 1))
            def _():
                pass_copy(1, c + d, c - 1, g).wait_send()

            for copy in result_copies(lax.rem(c + d, n), 0, lax.rem(c + d, n), g):
                copy.wait_send()

    for k in range(1, chips):
        node_copy(lax.rem(b + 2 * k, nb), b, n_send.at[k]).wait_send()
        node_pass(lax.rem(b + 2 * k, nb), n_pass.at[k]).wait_send()
    node_copy(twin, b, n_send.at[0]).wait_send()


def on_device(n, nb, prefix_kv, queries, new_kv, suffix_kv, suffix_len, node_kv, node_len, parent, leaf):
    rows = queries.shape[0] * GROUP
    dma = pltpu.SemaphoreType.DMA
    bf16, f32 = jnp.bfloat16, jnp.float32
    return pl.pallas_call(
        functools.partial(kernel, n, nb),
        out_shape=jax.ShapeDtypeStruct(queries.shape, bf16),
        in_specs=[pl.BlockSpec(memory_space=pltpu.HBM)] * 9,
        out_specs=pl.BlockSpec(memory_space=pltpu.VMEM),
        scratch_shapes=[
            pltpu.SMEM(suffix_len.shape, jnp.int32),
            pltpu.SMEM(node_len.shape, jnp.int32),
            pltpu.SMEM(parent.shape, jnp.int32),
            pltpu.SMEM(leaf.shape, jnp.int32),
            pltpu.VMEM(new_kv.shape, bf16),
            pltpu.VMEM(prefix_kv.shape, bf16),
            pltpu.VMEM(suffix_kv.shape, bf16),
            pltpu.VMEM((nb,) + node_kv.shape, bf16),
            pltpu.VMEM((KV_HEADS, HEAD_DIM, prefix_kv.shape[1]), bf16),
            pltpu.VMEM((n,) + queries.shape, bf16),
            pltpu.VMEM((n, KV_HEADS, HEAD_DIM, rows), f32),
            pltpu.VMEM((n, KV_HEADS, 1, rows), f32),
            pltpu.VMEM((n, KV_HEADS, HEAD_DIM, rows), bf16),
            pltpu.VMEM((n, KV_HEADS, 1, rows), f32),
            pltpu.VMEM((2, n, KV_HEADS, HEAD_DIM, rows), bf16),
            pltpu.VMEM((2, n, KV_HEADS, 1, rows), f32),
            pltpu.VMEM((2, KV_HEADS, HEAD_DIM, rows), f32),
            pltpu.VMEM((2, KV_HEADS, 1, rows), f32),
            dma((9,)),
            dma((2, n, KV_HEADS)),
            dma((n, KV_HEADS)),
            dma((n, KV_HEADS)),
            dma((2, n, KV_HEADS)),
            dma((n, KV_HEADS)),
            dma((2, n, KV_HEADS)),
            dma((nb // 2,)),
            dma((nb // 2,)),
            dma((nb,)),
        ],
        compiler_params=pltpu.CompilerParams(
            collective_id=0, has_side_effects=True, vmem_limit_bytes=63 * 1024 * 1024),
    )(suffix_len, node_len, parent, leaf, queries, new_kv, prefix_kv, suffix_kv, node_kv)


def solution(mesh):
    return jax.shard_map(
        functools.partial(on_device, mesh.shape["ctx"], mesh.shape["branch"]),
        mesh=mesh,
        in_specs=(
            P(None, ("parts", "ctx"), None),
            P(("parts", "ctx", "branch"), None),
            P(None, ("parts", "ctx", "branch"), None),
            P(None, ("parts", "ctx", "branch"), None, None),
            P(("parts", "ctx", "branch")),
            P(None, ("parts", "branch"), None, None),
            P("parts"),
            P("parts"),
            P(("parts", "ctx", "branch")),
        ),
        out_specs=P(("parts", "ctx", "branch"), None),
        check_vma=False,
    )
```

time: 57.2 us -> 51.8 us (0.906)
  the two profiles are of different devices: /device:TPU:1 before, /device:TPU:0 now
where the time goes in v2:
time: 51.8 us; the launch traced here: 51.5 us
  Pallas kernels  49.9 us (96%)
  local copies, waits for them, and re-layouts  1.67 us (3%)
    pallas_call x1, Pallas kernels, on_device(): pl.pallas_call(functools.partial(kernel, n, nb), out_shape=jax.ShapeDtype...  49.9 us
    unnamed x1, local copies, waits for them, and re-layouts  1.67 us

profile of v2, /device:TPU:0, one launch (start us, length us, event | category | flops | bytes accessed | tf_op | source)
XLA Modules:
  0.0 51.5 jit_solution(15454684604295934785)
XLA Ops:
  0.0 49.9 %shard_map.91 = bf16[16,8192]{1,0:T(8,128)(2,1)} custom-call(s32[16]{0:T(128)} %suffix_len_hbm.1, s32[4]{0:T(128)} %node_len_hbm.1, s32[4]{0:T(128)} %parent_hbm.1, s32[16]{0:T(128)} %leaf_hbm.1, bf16[16,8192]{1,0:T(8,128)(2,1)} %q_hbm.1, bf16[2,16,1024]{2,1,0:T(8,128)(2,1)} %new_hbm.1, bf16[2,1024,1024]{2,1,0:T(8,128)(2,1)} %prefix_hbm.1, ...), custom_call_target="tpu_custom_call" | custom-call | tf_op jit(solution)/shard_map/pallas_call | solution.py:351
  49.9 1.7 %copy.11 = bf16[16,8192]{1,0:T(8,128)(2,1)} copy(bf16[16,8192]{1,0:T(8,128)(2,1)} %shard_map.91) | data formatting | bytes 524288

commit v3 on v2

--- a/solution.py
+++ b/solution.py
@@ -21,7 +21,8 @@
 
 def dot_t(keys, rows):
     return lax.dot_general(keys, rows, (((1,), (1,)), ((), ())), preferred_element_type=jnp.float32)
-LAG = 2
+LAG = 4
+STEP = 4
 
 
 def kernel(
@@ -52,11 +53,25 @@
         load.start()
 
     barrier = pltpu.get_barrier_semaphore()
-    for k in range(1, n):
-        pl.semaphore_signal(barrier, inc=1, device_id={"ctx": lax.rem(c + k, n)}, device_id_type=MESH)
-    for k in range(1, nb):
-        pl.semaphore_signal(barrier, inc=1, device_id={"branch": lax.rem(b + k, nb)}, device_id_type=MESH)
-    pl.semaphore_wait(barrier, n - 1 + nb - 1)
+    @pl.when(c + 1 < n)
+    def _():
+        pl.semaphore_signal(barrier, inc=1, device_id={"ctx": c + 1}, device_id_type=MESH)
+
+    @pl.when(c >= 1)
+    def _():
+        pl.semaphore_signal(barrier, inc=1, device_id={"ctx": c - 1}, device_id_type=MESH)
+
+    pl.semaphore_signal(barrier, inc=1, device_id={"branch": twin}, device_id_type=MESH)
+    for k in range(1, chips):
+        pl.semaphore_signal(barrier, inc=1, device_id={"branch": lax.rem(b + 2 * k, nb)}, device_id_type=MESH)
+
+    @pl.when((c >= 1) & (c + 1 < n))
+    def _():
+        pl.semaphore_wait(barrier, chips + 2)
+
+    @pl.when((c == 0) | (c == n - 1))
+    def _():
+        pl.semaphore_wait(barrier, chips + 1)
 
     def cols(g):
         return pl.ds(pl.multiple_of(g * GW, GW), GW)
@@ -183,9 +198,6 @@
             l_part[dest, g] = stat
 
     def pair_item(pair, g):
-        for d in (2 * pair, 2 * pair + 1):
-            if d:
-                pump(d, g)
         one, two = (ranked(2 * pair) if pair else c), ranked(2 * pair + 1)
         query = jnp.concatenate(stack(qg[one, :, cols(g)]) + stack(qg[two, :, cols(g)]), axis=0)
         if pair == 0:
@@ -243,16 +255,24 @@
 
     loads[0].wait()
     loads[1].wait()
-    for pair in range(n // 2 - 1):
-        @pl.loop(0, KV_HEADS)
-        def _(g):
-            pair_item(pair, g)
-
-    @pl.loop(0, max(2 * KV_HEADS, KV_HEADS + LAG * (n - 2)))
-    def _(t):
-        @pl.when(t < KV_HEADS)
-        def _():
-            pair_item(n // 2 - 1, t)
+    tail = KV_HEADS * (n // 2 - 1)
+
+    @pl.loop(0, tail + max(2 * KV_HEADS, KV_HEADS + LAG * (n - 2)))
+    def _(time):
+        t = time - tail
+        for d in range(1, n):
+            ahead = time - STEP * (d - 1)
+
+            @pl.when((ahead >= 0) & (ahead < KV_HEADS))
+            def _():
+                pump(d, ahead)
+
+        for pair in range(n // 2):
+            turn = time - KV_HEADS * pair
+
+            @pl.when((turn >= 0) & (turn < KV_HEADS))
+            def _():
+                pair_item(pair, turn)
 
         for ring in range(1, n - 1):
             g = t - LAG * ring

time: 51.8 us -> 42.7 us (0.82)
  Pallas kernels: 49.9 us -> 40.9 us
    pallas_call x1, Pallas kernels: 49.9 us -> 40.9 us  [on_device(): pl.pallas_call(functools.partial(kernel, n, nb), out_shape=jax.ShapeDtype...]
where the time goes in v3:
time: 42.7 us; the launch traced here: 42.6 us
  Pallas kernels  40.9 us (96%)
  local copies, waits for them, and re-layouts  1.67 us (4%)
    pallas_call x1, Pallas kernels, on_device(): pl.pallas_call(functools.partial(kernel, n, nb), out_shape=jax.ShapeDtype...  40.9 us
    unnamed x1, local copies, waits for them, and re-layouts  1.67 us

profile of v3, /device:TPU:0, one launch (start us, length us, event | category | flops | bytes accessed | tf_op | source)
XLA Modules:
  0.0 42.6 jit_solution(1234978706796934183)
XLA Ops:
  0.0 40.9 %shard_map.91 = bf16[16,8192]{1,0:T(8,128)(2,1)} custom-call(s32[16]{0:T(128)} %suffix_len_hbm.1, s32[4]{0:T(128)} %node_len_hbm.1, s32[4]{0:T(128)} %parent_hbm.1, s32[16]{0:T(128)} %leaf_hbm.1, bf16[16,8192]{1,0:T(8,128)(2,1)} %q_hbm.1, bf16[2,16,1024]{2,1,0:T(8,128)(2,1)} %new_hbm.1, bf16[2,1024,1024]{2,1,0:T(8,128)(2,1)} %prefix_hbm.1, ...), custom_call_target="tpu_custom_call" | custom-call | tf_op jit(solution)/shard_map/pallas_call | solution.py:371
  40.9 1.7 %copy.11 = bf16[16,8192]{1,0:T(8,128)(2,1)} copy(bf16[16,8192]{1,0:T(8,128)(2,1)} %shard_map.91) | data formatting | bytes 524288

commit v4 on v3

--- a/solution.py
+++ b/solution.py
@@ -42,6 +42,19 @@
     core = lax.rem(b, 2)
     twin = b + 1 - 2 * core
 
+    barrier = pltpu.get_barrier_semaphore()
+    @pl.when(c + 1 < n)
+    def _():
+        pl.semaphore_signal(barrier, inc=1, device_id={"ctx": c + 1}, device_id_type=MESH)
+
+    @pl.when(c >= 1)
+    def _():
+        pl.semaphore_signal(barrier, inc=1, device_id={"ctx": c - 1}, device_id_type=MESH)
+
+    pl.semaphore_signal(barrier, inc=1, device_id={"branch": twin}, device_id_type=MESH)
+    for k in range(1, chips):
+        pl.semaphore_signal(barrier, inc=1, device_id={"branch": lax.rem(b + 2 * k, nb)}, device_id_type=MESH)
+
     loads = [
         pltpu.make_async_copy(src, dst, load_sem.at[i])
         for i, (src, dst) in enumerate([
@@ -51,19 +64,6 @@
     ]
     for load in loads:
         load.start()
-
-    barrier = pltpu.get_barrier_semaphore()
-    @pl.when(c + 1 < n)
-    def _():
-        pl.semaphore_signal(barrier, inc=1, device_id={"ctx": c + 1}, device_id_type=MESH)
-
-    @pl.when(c >= 1)
-    def _():
-        pl.semaphore_signal(barrier, inc=1, device_id={"ctx": c - 1}, device_id_type=MESH)
-
-    pl.semaphore_signal(barrier, inc=1, device_id={"branch": twin}, device_id_type=MESH)
-    for k in range(1, chips):
-        pl.semaphore_signal(barrier, inc=1, device_id={"branch": lax.rem(b + 2 * k, nb)}, device_id_type=MESH)
 
     @pl.when((c >= 1) & (c + 1 < n))
     def _():
@@ -209,12 +209,12 @@
         mixed = jnp.dot(vt[g], weights.astype(jnp.bfloat16), preferred_element_type=jnp.float32)
         mixed = mixed * (1.0 / total)
         stat = peak + jnp.log2(total)
+        emit(two, g, mixed[:, rows:], stat[:, rows:])
         if pair:
             emit(one, g, mixed[:, :rows], stat[:, :rows])
         else:
             o_loc[0, g] = mixed[:, :rows]
             l_loc[0, g] = stat[:, :rows]
-        emit(two, g, mixed[:, rows:], stat[:, rows:])
 
     def merge(dest, side, g):
         for copy in result_copies(dest, side, dest, g):
@@ -286,7 +286,7 @@
 
                 @pl.when(c == ring)
                 def _():
-                    for dest in range(ring + 1, n):
+                    for dest in range(n - 1, ring, -1):
                         merge(dest, 1, g)
 
         @pl.when(t == KV_HEADS - 2)

time: 42.7 us -> 42.7 us (level)
  no operation moved by 1% of the time
where the time goes in v4:
time: 42.7 us; the launch traced here: 42.5 us
  Pallas kernels  40.9 us (96%)
  local copies, waits for them, and re-layouts  1.67 us (4%)
    pallas_call x1, Pallas kernels, on_device(): pl.pallas_call(functools.partial(kernel, n, nb), out_shape=jax.ShapeDtype...  40.9 us
    unnamed x1, local copies, waits for them, and re-layouts  1.67 us

profile of v4, /device:TPU:0, one launch (start us, length us, event | category | flops | bytes accessed | tf_op | source)
XLA Modules:
  0.0 42.5 jit_solution(2335856966994227844)
XLA Ops:
  0.0 40.9 %shard_map.91 = bf16[16,8192]{1,0:T(8,128)(2,1)} custom-call(s32[16]{0:T(128)} %suffix_len_hbm.1, s32[4]{0:T(128)} %node_len_hbm.1, s32[4]{0:T(128)} %parent_hbm.1, s32[16]{0:T(128)} %leaf_hbm.1, bf16[16,8192]{1,0:T(8,128)(2,1)} %q_hbm.1, bf16[2,16,1024]{2,1,0:T(8,128)(2,1)} %new_hbm.1, bf16[2,1024,1024]{2,1,0:T(8,128)(2,1)} %prefix_hbm.1, ...), custom_call_target="tpu_custom_call" | custom-call | tf_op jit(solution)/shard_map/pallas_call | solution.py:371
  40.9 1.7 %copy.11 = bf16[16,8192]{1,0:T(8,128)(2,1)} copy(bf16[16,8192]{1,0:T(8,128)(2,1)} %shard_map.91) | data formatting | bytes 524288
